TPU v7x, 32 devices: a whole 2x2x4 slice. The times are simulated.
32 devices in a mesh: cols: 4 (over y, x), rows: 8 (over z, core).
Axes of the slice: x: 2, y: 2, z: 4, core: 2. Of those that a mesh axis runs over, the one named last changes fastest.
Arguments:
- gradient: float32 [128, 8192], P('cols', 'rows'), may hold values from -100 to 100
- width_factor: float32 [128, 128], P(None, 'cols'), may hold values from -3 to 4, as said below
- diag_blocks: float32 [64, 128, 128], P('rows'), may hold values from -2 to 24, as said below
- jacobi_inverse: float32 [64, 128, 128], P('rows'), may hold values from -2 to 2, as said below
- coupling_tiles: bfloat16 [32, 128, 128], P('rows'), may hold values from -4 to 4, as said below
- tile_local: int32 [32], P('rows'), may hold values from 0 to 7
- tile_remote: int32 [32], P('rows'), may hold values from 0 to 63, as said below
- tile_count: int32 [8], P('rows'), may hold values from 0 to 3, as said below
Outputs:
- solution: float32 [128, 8192], P('cols', 'rows')
- residual: float32 [128, 8192], P('cols', 'rows')
Inputs may be any that keep to these rules, and one draw needn't show every extreme that they name: `tile_remote`: the live entries are the first tile_count entries of each device's list; they name distinct devices other than the owner, each at most once. For a live entry of device d naming block J of device e, device e has a live entry naming d's block with its tile the transpose. Pad entries hold valid indices. `tile_count`: at most 3 on one device, reached on some device. `coupling_tiles`: with diag_blocks and the live entries, M is symmetric positive definite. `diag_blocks`: symmetric positive definite tiles. `jacobi_inverse`: the inverses of diag_blocks, symmetric. `width_factor`: symmetric positive definite.
All inputs are finite; a program needn't handle non-finite values.
Results may differ from a plain program's by a relative error of at most 0.0085.
Values may be sent and summed in bfloat16 or wider, within the bound.
No kernel may reach another device: no remote copies, remote signals or barrier semaphores. Data moves between devices by JAX's collectives and lax.ppermute only.
A program may use at most 64 MiB of HBM per device.

v0:
```python
import jax
import jax.numpy as jnp
from jax import lax
from jax.sharding import PartitionSpec as P

BLOCK = 128
ITERS = 6


highest = lax.Precision.HIGHEST


def on_device(
    gradient,
    width_factor,
    diag_blocks,
    jacobi_inverse,
    coupling_tiles,
    tile_local,
    tile_remote,
    tile_count,
):
    width_dev, rows_dev = gradient.shape
    blocks_dev = diag_blocks.shape[0]
    slot_count = tile_local.shape[0]
    devices = lax.axis_size("rows")
    active_slot = jnp.arange(slot_count, dtype=jnp.int32) < tile_count[0]
    placing = (
        (tile_local[:, None] == jnp.arange(blocks_dev, dtype=jnp.int32)[None, :])
        & active_slot[:, None]
    ).astype(jnp.float32)
    owner_dev = tile_remote // blocks_dev
    matches = active_slot[:, None] & (
        owner_dev[:, None] == jnp.arange(devices, dtype=jnp.int32)[None, :]
    )
    request = jnp.sum(jnp.where(matches, (tile_remote % blocks_dev)[:, None], 0), axis=0)
    granted = lax.all_to_all(request, "rows", split_axis=0, concat_axis=0, tiled=True)

    def precondition(vector):
        blocks = vector.reshape(width_dev, blocks_dev, BLOCK)
        return jnp.einsum("enj,nji->eni", blocks, jacobi_inverse, precision=highest).reshape(
            width_dev, rows_dev
        )

    solution = jnp.zeros_like(gradient)
    residual = gradient
    precond_res = precondition(residual)
    direction = precond_res
    res_norm = lax.psum(jnp.sum(residual * precond_res), ("cols", "rows"))
    for iteration in range(ITERS):
        apply_blocks = direction.reshape(width_dev, blocks_dev, BLOCK)
        local_part = jnp.einsum("enj,nji->eni", apply_blocks, diag_blocks, precision=highest)
        rounded = direction.astype(jnp.bfloat16).reshape(width_dev, blocks_dev, BLOCK)
        incoming = lax.all_to_all(
            rounded[:, granted, :], "rows", split_axis=1, concat_axis=1, tiled=True
        )
        sources = incoming[:, owner_dev, :]
        products = jnp.einsum(
            "ekj,kji->eki", sources, coupling_tiles, preferred_element_type=jnp.float32
        )
        coupled = jnp.einsum("eki,kb->ebi", products, placing, precision=highest)
        summed = lax.psum(
            jnp.dot(
                width_factor, (local_part + coupled).reshape(width_dev, rows_dev), precision=highest
            ),
            "cols",
        )
        fisher_dir = lax.dynamic_slice_in_dim(
            summed, lax.axis_index("cols") * width_dev, width_dev, 0
        )
        precond_fisher = precondition(fisher_dir)
        curvature, cross_term, second_term = lax.psum(
            (
                jnp.sum(direction * fisher_dir),
                jnp.sum(fisher_dir * precond_res),
                jnp.sum(fisher_dir * precond_fisher),
            ),
            ("cols", "rows"),
        )
        step_size = res_norm / curvature
        solution = solution + step_size * direction
        residual = residual - step_size * fisher_dir
        if iteration + 1 < ITERS:
            precond_res = precond_res - step_size * precond_fisher
            next_norm = (
                res_norm - 2.0 * step_size * cross_term + step_size * step_size * second_term
            )
            direction = precond_res + next_norm / res_norm * direction
            res_norm = next_norm
    return (solution, residual)


def solution(mesh):
    placed = (
        P("cols", "rows"),
        P(None, "cols"),
        P("rows", None, None),
        P("rows", None, None),
        P("rows", None, None),
        P("rows"),
        P("rows"),
        P("rows"),
    )
    return jax.shard_map(
        on_device,
        mesh=mesh,
        in_specs=placed,
        out_specs=(P("cols", "rows"), P("cols", "rows")),
        check_vma=False,
    )
```

profile of v0, /device:TPU:0, one launch (start us, length us, event | category | flops | bytes accessed | tf_op | source)
XLA Modules:
  0.0 644.4 jit_solution(5383939424549361704)
XLA Ops:
  9.3 6.4 all-to-all-start
  15.7 1.5 bitcast_convert_fusion
  17.2 4.0 all-to-all-done
  22.6 3.4 all-to-all-start.1
  26.1 5.7 all-to-all-done.1
  35.1 44.0 %all-reduce.12.cloned.1.call-done = f32[128,1024]{1,0:T(8,128)} async-done(((f32[128,1024]{1,0:T(8,128)}), f32[128,1024]{1,0:T(8,128)}) %all-reduce.12.cloned.1.call-update) | async-done | bytes 524304 | tf_op jit(solution)/shard_map/psum | solution.py:62
  79.0 1.5 fusion.49
  80.5 1.6 fusion.25
  82.1 39.6 %all-reduce.4 = (f32[]{:T(128)}, f32[]{:T(128)}, f32[]{:T(128)}) all-reduce(f32[]{:T(128)} %get-tuple-element.24, f32[]{:T(128)} %get-tuple-element.23, f32[]{:T(128)} %get-tuple-element.22), channel_id=1, replica_groups=mesh['cols'=4,'rows'=8] {'cols','rows'}, use_global_device_ids=true, to_apply=%region_1.2 | all-reduce | flops 3 | bytes 24 | tf_op jit(solution)/shard_map/psum | solution.py:49
  126.0 9.3 %all_to_all.42 = bf16[32,8,128]{2,0,1:T(8,128)(2,1)S(1)} all-to-all(bf16[32,8,128]{2,0,1:T(8,128)(2,1)S(1)} %bitcast.343), channel_id=1, replica_groups=mesh['cols'=4,'rows'=8] {'rows'}, dimensions={1} | all-to-all | bytes 131072 | tf_op jit(solution)/shard_map/all_to_all | solution.py:54
  138.4 45.0 %all-reduce.14.cloned.1.call-done = f32[128,1024]{1,0:T(8,128)} async-done(((f32[128,1024]{1,0:T(8,128)}), f32[128,1024]{1,0:T(8,128)}) %all-reduce.14.cloned.1.call-update) | async-done | bytes 524304 | tf_op jit(solution)/shard_map/psum | solution.py:62
  183.4 1.5 fusion.46
  185.7 39.6 %all-reduce.3 = (f32[]{:T(128)}, f32[]{:T(128)}, f32[]{:T(128)}) all-reduce(f32[]{:T(128)} %get-tuple-element.21, f32[]{:T(128)} %get-tuple-element.20, f32[]{:T(128)} %get-tuple-element.19), channel_id=1, replica_groups=mesh['cols'=4,'rows'=8] {'cols','rows'}, use_global_device_ids=true, to_apply=%region_10.11 | all-reduce | flops 3 | bytes 24 | tf_op jit(solution)/shard_map/psum | solution.py:72
  227.8 9.3 %all_to_all.43 = bf16[32,8,128]{2,0,1:T(8,128)(2,1)S(1)} all-to-all(bf16[32,8,128]{2,0,1:T(8,128)(2,1)S(1)} %bitcast.344), channel_id=1, replica_groups=mesh['cols'=4,'rows'=8] {'rows'}, dimensions={1} | all-to-all | bytes 131072 | tf_op jit(solution)/shard_map/all_to_all | solution.py:54
  240.2 45.0 %all-reduce.16.cloned.1.call-done = f32[128,1024]{1,0:T(8,128)} async-done(((f32[128,1024]{1,0:T(8,128)}), f32[128,1024]{1,0:T(8,128)}) %all-reduce.16.cloned.1.call-update) | async-done | bytes 524304 | tf_op jit(solution)/shard_map/psum | solution.py:62
  285.2 1.5 fusion.43
  286.6 1.7 multiply_reduce_fusion.5
  288.3 39.6 %all-reduce.2 = (f32[]{:T(128)}, f32[]{:T(128)}, f32[]{:T(128)}) all-reduce(f32[]{:T(128)} %get-tuple-element.13, f32[]{:T(128)} %get-tuple-element.12, f32[]{:T(128)} %get-tuple-element.18), channel_id=1, replica_groups=mesh['cols'=4,'rows'=8] {'cols','rows'}, use_global_device_ids=true, to_apply=%region_17.18 | all-reduce | flops 3 | bytes 24 | tf_op jit(solution)/shard_map/psum | solution.py:72
  330.4 9.3 %all_to_all.44 = bf16[32,8,128]{2,0,1:T(8,128)(2,1)S(1)} all-to-all(bf16[32,8,128]{2,0,1:T(8,128)(2,1)S(1)} %bitcast.345), channel_id=1, replica_groups=mesh['cols'=4,'rows'=8] {'rows'}, dimensions={1} | all-to-all | bytes 131072 | tf_op jit(solution)/shard_map/all_to_all | solution.py:54
  342.8 45.0 %all-reduce.18.cloned.1.call-done = f32[128,1024]{1,0:T(8,128)} async-done(((f32[128,1024]{1,0:T(8,128)}), f32[128,1024]{1,0:T(8,128)}) %all-reduce.18.cloned.1.call-update) | async-done | bytes 524304 | tf_op jit(solution)/shard_map/psum | solution.py:62
  389.2 1.6 fusion.13
  390.8 39.7 %all-reduce.1 = (f32[]{:T(128)}, f32[]{:T(128)}, f32[]{:T(128)}) all-reduce(f32[]{:T(128)} %get-tuple-element.17, f32[]{:T(128)} %get-tuple-element.16, f32[]{:T(128)} %get-tuple-element.15), channel_id=1, replica_groups=mesh['cols'=4,'rows'=8] {'cols','rows'}, use_global_device_ids=true, to_apply=%region_24.25 | all-reduce | flops 3 | bytes 24 | tf_op jit(solution)/shard_map/psum | solution.py:72
  433.2 9.3 %all_to_all.45 = bf16[32,8,128]{2,0,1:T(8,128)(2,1)S(1)} all-to-all(bf16[32,8,128]{2,0,1:T(8,128)(2,1)S(1)} %bitcast.346), channel_id=1, replica_groups=mesh['cols'=4,'rows'=8] {'rows'}, dimensions={1} | all-to-all | bytes 131072 | tf_op jit(solution)/shard_map/all_to_all | solution.py:54
  445.5 45.1 %all-reduce.20.cloned.1.call-done = f32[128,1024]{1,0:T(8,128)} async-done(((f32[128,1024]{1,0:T(8,128)}), f32[128,1024]{1,0:T(8,128)}) %all-reduce.20.cloned.1.call-update) | async-done | bytes 524304 | tf_op jit(solution)/shard_map/psum | solution.py:62
  490.6 1.5 fusion.37
  492.1 1.6 multiply_reduce_fusion.1
  493.6 39.6 %all-reduce = (f32[]{:T(128)}, f32[]{:T(128)}, f32[]{:T(128)}) all-reduce(f32[]{:T(128)} %get-tuple-element.11, f32[]{:T(128)} %get-tuple-element.10, f32[]{:T(128)} %get-tuple-element.14), channel_id=1, replica_groups=mesh['cols'=4,'rows'=8] {'cols','rows'}, use_global_device_ids=true, to_apply=%region_31.32 | all-reduce | flops 3 | bytes 24 | tf_op jit(solution)/shard_map/psum | solution.py:72
  535.8 9.3 %all_to_all.46 = bf16[32,8,128]{2,0,1:T(8,128)(2,1)S(1)} all-to-all(bf16[32,8,128]{2,0,1:T(8,128)(2,1)S(1)} %bitcast.342), channel_id=1, replica_groups=mesh['cols'=4,'rows'=8] {'rows'}, dimensions={1} | all-to-all | bytes 131072 | tf_op jit(solution)/shard_map/all_to_all | solution.py:54
  548.1 45.1 %all-reduce.22.cloned.1.call-done = f32[128,1024]{1,0:T(8,128)} async-done(((f32[128,1024]{1,0:T(8,128)}), f32[128,1024]{1,0:T(8,128)}) %all-reduce.22.cloned.1.call-update) | async-done | bytes 524304 | tf_op jit(solution)/shard_map/psum | solution.py:62
  593.2 1.5 multiply_reduce_fusion
  594.7 39.5 %psum.178 = f32[]{:T(128)} all-reduce(f32[]{:T(128)} %multiply_reduce_fusion), channel_id=1, replica_groups=mesh['cols'=4,'rows'=8] {'cols','rows'}, use_global_device_ids=true, to_apply=%region_38.39 | all-reduce | flops 1 | bytes 8 | tf_op jit(solution)/shard_map/psum | solution.py:72
  635.7 1.9 multiply_subtract_fusion
  (81 shorter events, 27.2 us)
Async XLA Ops:
  7.2 8.5 %copy-start = (f32[8,128,128]{2,1,0:T(8,128)S(1)}, f32[8,128,128]{2,1,0:T(8,128)}, u32[]{:S(2)}) copy-start(f32[8,128,128]{2,1,0:T(8,128)} %param.11) | copy-start | bytes 1572868
  7.9 0.7 copy-start.6
  9.3 11.9 %all-to-all-start = ((s32[8,1,1]{2,1,0:T(1,128)}), s32[8,1,1]{2,1,0:T(1,128)S(1)}, u32[]{:S(2)}, u32[]{:S(2)}) async-start(s32[8,1,1]{2,1,0:T(1,128)} %copy.175), calls=%async_computation | async-start | bytes 8192 | tf_op jit(solution)/shard_map/all_to_all | solution.py:37
  15.7 10.4 %copy-start.7 = (s32[4]{0:T(128)S(1)}, s32[4]{0:T(128)}, u32[]{:S(2)}) copy-start(s32[4]{0:T(128)} %param.13) | copy-start | bytes 52
  15.7 16.7 %copy-start.2 = (bf16[4,128,128]{2,1,0:T(8,128)(2,1)S(1)}, bf16[4,128,128]{2,1,0:T(8,128)(2,1)}, u32[]{:S(2)}) copy-start(bf16[4,128,128]{2,1,0:T(8,128)(2,1)} %param.12) | copy-start | bytes 393220
  17.2 15.6 %copy-start.1 = (f32[8,128,128]{2,1,0:T(8,128)S(1)}, f32[8,128,128]{2,1,0:T(8,128)}, u32[]{:S(2)}) copy-start(f32[8,128,128]{2,1,0:T(8,128)} %param.10) | copy-start | bytes 1572868
  22.6 9.2 %all-to-all-start.1 = ((bf16[32,8,128]{2,0,1:T(8,128)(2,1)}), bf16[32,8,128]{2,0,1:T(8,128)(2,1)S(1)}, u32[]{:S(2)}, u32[]{:S(2)}) async-start(bf16[32,8,128]{2,0,1:T(8,128)(2,1)} %bitcast.5), calls=%async_computation.1 | async-start | bytes 131072 | tf_op jit(solution)/shard_map/all_to_all | solution.py:54
  26.0 53.0 %all-reduce.12.cloned.1.call-start = ((), (), s32[]{:S(2)}) async-start(), calls=%async_computation.7 | async-start | bytes 1048576 | tf_op jit(solution)/shard_map/psum | solution.py:62
  32.8 0.7 copy-start.4
  35.0 148.4 %all-reduce.14.cloned.1.call-start = ((), (), s32[]{:S(2)}) async-start(), calls=%async_computation.8 | async-start | bytes 1048576 | tf_op jit(solution)/shard_map/psum | solution.py:62
  35.1 45.4 %copy-start.3 = (f32[32,1024]{1,0:T(8,128)S(1)}, f32[32,1024]{1,0:T(8,128)}, u32[]{:S(2)}) copy-start(f32[32,1024]{1,0:T(8,128)} %param.8) | copy-start | bytes 393220
  138.3 146.9 %all-reduce.16.cloned.1.call-start = ((), (), s32[]{:S(2)}) async-start(), calls=%async_computation.9 | async-start | bytes 1048576 | tf_op jit(solution)/shard_map/psum | solution.py:62
  183.4 1.5 copy-start.5
  240.1 147.7 %all-reduce.18.cloned.1.call-start = ((), (), s32[]{:S(2)}) async-start(), calls=%async_computation.10 | async-start | bytes 1048576 | tf_op jit(solution)/shard_map/psum | solution.py:62
  342.7 147.9 %all-reduce.20.cloned.1.call-start = ((), (), s32[]{:S(2)}) async-start(), calls=%async_computation.11 | async-start | bytes 1048576 | tf_op jit(solution)/shard_map/psum | solution.py:62
  445.5 147.7 %all-reduce.22.cloned.1.call-start = ((), (), s32[]{:S(2)}) async-start(), calls=%async_computation.12 | async-start | bytes 1048576 | tf_op jit(solution)/shard_map/psum | solution.py:62
Sparse Core Ops, SparseCore 0:
  35.1 43.8 all-reduce.11
  138.4 44.9 all-reduce.13
  240.2 44.9 all-reduce.15
  342.8 44.8 all-reduce.17
  445.6 44.9 all-reduce.19
  548.2 44.9 all-reduce.21
where the time goes:
time: 646 us; the launch traced here: 644 us
  blocking collectives  284 us (44%)
  waiting for transfers between devices  279 us (43%)
  between operations  27.4 us (4%)
  matrix products  23.3 us (4%)
  other arithmetic  12 us (2%)
  starting transfers between devices  9.95 us (2%)
  local copies, waits for them, and re-layouts  8.86 us (1%)
    psum x6, waiting for transfers between devices, on_device(): lax.psum(jnp.dot(width_factor, (local_part + coupled).reshape(width_dev,...  269 us
    psum x5, blocking collectives, on_device(): lax.psum((jnp.sum(direction * fisher_dir), jnp.sum(fisher_dir * precond_r...  198 us
    all_to_all x5, blocking collectives, on_device(): lax.all_to_all(rounded[:, granted, :], 'rows', split_axis=1, concat_axis=...  46.4 us
    psum x1, blocking collectives, on_device(): res_norm = lax.psum(jnp.sum(residual * precond_res), ('cols', 'rows'))  39.6 us
  transfers between devices with their start and end apart: 8, of which 8 were waited for; matrix products, arithmetic and copies ran while one was open for 0% of the time, Pallas kernels for 0%

commit v1 on v0

v1 whole, which is shorter than its diff:
```python
import functools

import jax
import jax.numpy as jnp
from jax import lax
from jax.experimental import pallas as pl
from jax.experimental.pallas import tpu as pltpu
from jax.sharding import PartitionSpec as P

BLOCK = 128
ITERS = 6
STRETCH = 1.1
GATHER_BYTES = 8 * 2**20

highest = lax.Precision.HIGHEST
f32 = jnp.float32
VMEM = pl.BlockSpec(memory_space=pltpu.VMEM)
SMEM = pl.BlockSpec(memory_space=pltpu.SMEM)


def dot(a, b):
    return jnp.dot(a, b, precision=highest, preferred_element_type=f32)


def call(kernel, outs, *args, scalars=0, scratch=()):
    specs = [SMEM] * scalars + [VMEM] * (len(args) - scalars)
    many = isinstance(outs, tuple)
    return pl.pallas_call(
        kernel,
        out_shape=outs,
        in_specs=specs,
        out_specs=tuple([VMEM] * len(outs)) if many else VMEM,
        scratch_shapes=list(scratch),
    )(*args)


def split(x):
    high = x.astype(jnp.bfloat16)
    return high, (x - high.astype(f32)).astype(jnp.bfloat16)


def pack_kernel(local, gradient, jacobi, tiles, packed):
    for slot in range(packed.shape[0]):
        block = local[slot]
        tile = tiles[slot].astype(f32)
        packed[slot, :BLOCK, :] = lax.dot_general(
            jacobi[block],
            tile,
            (((1,), (1,)), ((), ())),
            precision=highest,
            preferred_element_type=f32,
        )
        columns = pl.ds(pl.multiple_of(block * BLOCK, BLOCK), BLOCK)
        packed[slot, BLOCK:, :] = gradient[:, columns]


def chain_kernel(sources, near, far, chain, high, low, held, out):
    groups, slots = near.shape[:2]
    half = groups * slots
    total = 2 * half
    width = near.shape[2] - BLOCK
    for q in range(total):
        ref = near if q < half else far
        group, slot = divmod(q % half, slots)
        high[q], low[q] = split(ref[group, slot, :BLOCK, :])
        held[q] = ref[group, slot, BLOCK:, :]
    out[total] = jnp.zeros((width, BLOCK), f32)

    def step(j, carry):
        for q in range(total):
            first, second = split(held[q])
            both = jnp.dot(
                jnp.concatenate([first, second], 0), high[q], preferred_element_type=f32
            )
            rest = jnp.dot(first, low[q], preferred_element_type=f32)
            out[q] = both[:width] + both[width:] + rest
        for q in range(total):
            value = out[sources[q * slots]]
            for i in range(1, slots):
                value += out[sources[q * slots + i]]
            held[q] = value
        for slot in range(slots):
            chain[j, slot] = held[slot]
        return carry

    lax.fori_loop(0, ITERS, step, 0)


def shift(x, axis, by):
    size = lax.axis_size(axis)
    return lax.ppermute(x, axis, [(i, (i - by) % size) for i in range(size)])


def chain_gathered(gradient, jacobi, tiles, local, remote, live):
    width = gradient.shape[0]
    blocks, slots = jacobi.shape[0], local.shape[0]
    devices = lax.axis_size("rows")
    groups = devices // 2
    packed = call(
        pack_kernel,
        jax.ShapeDtypeStruct((slots, BLOCK + width, BLOCK), f32),
        local,
        gradient,
        jacobi,
        tiles,
        scalars=1,
    )
    near = jnp.stack([packed] + [shift(packed, "rows", 2 * o) for o in range(1, groups)])
    far = lax.ppermute(near, "rows", [(i, i ^ 1) for i in range(devices)])

    own = jnp.concatenate([local, remote, live.astype(jnp.int32)])
    own = jnp.pad(own, (0, BLOCK - own.shape[0]))
    told = jnp.broadcast_to(own[None, None, :], (devices, 1, BLOCK))
    told = lax.all_to_all(told, "rows", 0, 0, tiled=True)[:, 0]
    me = lax.axis_index("rows")
    position = jnp.arange(devices, dtype=jnp.int32)
    base = me ^ (position // groups)
    device = (base + 2 * (position % groups)) % devices
    pick = (device[:, None] == jnp.arange(devices, dtype=jnp.int32)[None, :]).astype(jnp.int32)
    told = jnp.sum(pick[:, :, None] * told[None, :, :], axis=1)
    locals_, remotes, lives = (
        told[:, i * slots : (i + 1) * slots] for i in range(3)
    )
    owner = (remotes // blocks).reshape(-1)
    holder = jnp.broadcast_to(device[:, None], locals_.shape).reshape(-1)
    alive = lives.reshape(-1) > 0
    meets = (
        (owner[:, None] == holder[None, :])
        & (owner[None, :] == holder[:, None])
        & alive[None, :]
    )
    total = devices * slots
    numbers = jnp.arange(total, dtype=jnp.int32)
    partner = jnp.sum(jnp.where(meets, numbers[None, :], 0), axis=1).reshape(devices, slots)
    same = (
        (locals_[:, :, None] == locals_[:, None, :])
        & (lives[:, None, :] > 0)
        & (lives[:, :, None] > 0)
    )
    sources = jnp.where(same, partner[:, None, :], total).reshape(-1)
    return call(
        chain_kernel,
        jax.ShapeDtypeStruct((ITERS, slots, width, BLOCK), f32),
        sources,
        near,
        far,
        scalars=1,
        scratch=[
            pltpu.VMEM((total, BLOCK, BLOCK), jnp.bfloat16),
            pltpu.VMEM((total, BLOCK, BLOCK), jnp.bfloat16),
            pltpu.VMEM((total, width, BLOCK), f32),
            pltpu.VMEM((total + 1, width, BLOCK), f32),
        ],
    )


def chain_exchanged(gradient, jacobi, tiles, local, remote, live):
    width = gradient.shape[0]
    blocks = jacobi.shape[0]
    devices = lax.axis_size("rows")
    owner = remote // blocks
    placing = (
        (local[:, None] == jnp.arange(blocks, dtype=jnp.int32)[None, :]) & live[:, None]
    ).astype(f32)
    meets = live[:, None] & (owner[:, None] == jnp.arange(devices, dtype=jnp.int32)[None, :])
    granted = jnp.sum(jnp.where(meets, local[:, None], 0), axis=0)
    vector = jnp.transpose(gradient.reshape(width, blocks, BLOCK), (1, 0, 2))
    steps = []
    for _ in range(ITERS):
        sent = jnp.einsum("nej,nji->nei", vector, jacobi, precision=highest)[granted]
        incoming = lax.all_to_all(sent, "rows", 0, 0, tiled=True)
        products = jnp.einsum(
            "kej,kji->kei", incoming[owner], tiles.astype(f32), precision=highest
        )
        vector = jnp.einsum("kei,kn->nei", products, placing, precision=highest)
        steps.append(vector)
    return jnp.stack(steps)


def basis_kernel(turn, *refs):
    devices = len(refs) - 5
    pieces, jacobi = refs[:devices], refs[devices]
    mixes, plain, smooth, scale = refs[devices + 1 :]
    width = pieces[0].shape[0]
    blocks = jacobi.shape[0]
    rows = blocks * BLOCK
    factor = jnp.concatenate([piece[:, rows:] for piece in pieces], 0)
    factor = pltpu.roll(factor, turn[0], 1)
    norm = jnp.max(jnp.sum(jnp.abs(factor), axis=1, keepdims=True), axis=0, keepdims=True)
    power = factor / norm
    for _ in range(3):
        power = dot(power, power)
    bound = jnp.sum(jnp.sum(power * power, axis=1, keepdims=True), axis=0, keepdims=True)
    for _ in range(4):
        bound = jnp.sqrt(bound)
    ratio = 2.0 / (STRETCH * bound * norm)
    scale[...] = jnp.broadcast_to(ratio, scale.shape)
    factor = factor * ratio

    row = lax.broadcasted_iota(jnp.int32, (width, BLOCK), 0)
    lane = lax.broadcasted_iota(jnp.int32, (width, BLOCK), 1)
    kept = [[(row == lane).astype(f32)]]
    for k in range(ITERS):
        last = kept[k]
        terms = [last[0]] + [last[j] + last[j - 1] for j in range(1, k + 1)] + [last[k]]
        image = dot(jnp.concatenate(terms, 0), factor)
        fresh = []
        for j in range(k + 2):
            value = image[j * width : (j + 1) * width]
            if j <= k:
                value = value - last[j]
            if k:
                value = 2.0 * value
                if j <= k - 1:
                    value = value - kept[k - 1][j]
            fresh.append(value)
        kept.append(fresh)
    at = 0
    for j in range(1, ITERS + 1):
        for k in range(j, ITERS + 1):
            mixes[at : at + width, :] = kept[k][j]
            at += width
    first = jnp.concatenate([kept[k][0] for k in range(ITERS + 1)], 0)
    for b in range(blocks):
        columns = slice(b * BLOCK, (b + 1) * BLOCK)
        whole = jnp.concatenate([piece[:, columns] for piece in pieces], 0)
        value = dot(first, whole)
        plain[b] = value
        smooth[b] = dot(value[: ITERS * width], jacobi[b])


def mix_kernel(local, used, *refs):
    devices = len(refs) - 10
    chains = refs[:devices]
    gradient, mixes, plain, smooth, jacobi = refs[devices : devices + 5]
    images, precond, gram, basis, added = refs[devices + 5 :]
    slots, width = chains[0].shape[1:3]
    blocks = jacobi.shape[0]
    tall = ITERS * width
    basis[...] = plain[...]
    precond[...] = smooth[...]
    for slot in range(slots):
        added[...] = jnp.zeros(added.shape, f32)
        at = 0
        for j in range(1, ITERS + 1):
            count = (ITERS + 1 - j) * width
            whole = jnp.concatenate([chain[j - 1, slot] for chain in chains], 0)
            added[j * width :, :] += dot(mixes[at : at + count, :], whole)
            at += count

        @pl.when(used[slot] > 0)
        def _():
            block = local[slot]
            basis[block] += added[...]
            precond[block] += dot(added[:tall, :], jacobi[block])

    sums = {}
    for b in range(blocks):
        for r in range(0, width, 8):
            s = [basis[b, k * width + r : k * width + r + 8, :] for k in range(ITERS + 1)]
            y = [precond[b, k * width + r : k * width + r + 8, :] for k in range(ITERS)]
            g = gradient[r : r + 8, b * BLOCK : (b + 1) * BLOCK]
            f = [s[0] + s[1]]
            for j in range(1, ITERS):
                f.append(0.5 * (s[j - 1] + s[j + 1]) + s[j])
            for j in range(ITERS):
                images[b, j * width + r : j * width + r + 8, :] = f[j]
            for i in range(ITERS):
                for j in range(i + 1):
                    sums[i, j] = sums.get((i, j), 0.0) + y[i] * f[j]
                sums[i, ITERS] = sums.get((i, ITERS), 0.0) + y[i] * g
    lane = lax.broadcasted_iota(jnp.int32, (1, BLOCK), 1)
    result = jnp.zeros((1, BLOCK), f32)
    for (i, j), value in sums.items():
        value = jnp.sum(jnp.sum(value, axis=0, keepdims=True), axis=1, keepdims=True)
        here = lane == 16 * i + j
        if j < ITERS:
            here = here | (lane == 16 * j + i)
        result = jnp.where(here, value, result)
    gram[...] = result


def finish_kernel(grams, scale, gradient, precond, images, solution, residual):
    width = gradient.shape[0]
    blocks = precond.shape[0]
    flat = jnp.sum(grams[:, 0, :], axis=0, keepdims=True)
    row = lax.broadcasted_iota(jnp.int32, (8, BLOCK), 0)
    lane = lax.broadcasted_iota(jnp.int32, (8, BLOCK), 1)
    table = jnp.zeros((8, BLOCK), f32)
    for i in range(ITERS):
        moved = flat if i == 0 else pltpu.roll(flat, BLOCK - 16 * i, 1)
        table = jnp.where((row == i) & (lane <= ITERS), moved, table)
    for p in range(ITERS):
        pivot = table[p : p + 1, :] / table[p : p + 1, p : p + 1]
        table = jnp.where(row == p, pivot, table - table[:, p : p + 1] * pivot)
    steps = [table[j : j + 1, ITERS : ITERS + 1] for j in range(ITERS)]
    longer = scale[0:1, 0:1]
    for b in range(blocks):
        columns = slice(b * BLOCK, (b + 1) * BLOCK)
        total = steps[0] * precond[b, :width, :]
        left = gradient[:, columns] - steps[0] * images[b, :width, :]
        for j in range(1, ITERS):
            part = slice(j * width, (j + 1) * width)
            total = total + steps[j] * precond[b, part, :]
            left = left - steps[j] * images[b, part, :]
        solution[:, columns] = longer * total
        residual[:, columns] = left


def on_device(
    gradient,
    width_factor,
    diag_blocks,
    jacobi_inverse,
    coupling_tiles,
    tile_local,
    tile_remote,
    tile_count,
    exchange=False,
):
    width, rows = gradient.shape
    blocks = diag_blocks.shape[0]
    columns = lax.axis_size("cols")
    devices = lax.axis_size("rows")
    slots = tile_local.shape[0] - 1
    local, remote, tiles = tile_local[:slots], tile_remote[:slots], coupling_tiles[:slots]
    live = jnp.arange(slots, dtype=jnp.int32) < tile_count[0]

    piece = jnp.concatenate([gradient, width_factor.T], axis=1)
    pieces = [piece] + [shift(piece, "cols", o) for o in range(1, columns)]

    gathered = devices * slots * BLOCK * (BLOCK + width) * 4
    if gathered <= GATHER_BYTES and devices % 2 == 0 and not exchange:
        chain = chain_gathered(gradient, jacobi_inverse, tiles, local, remote, live)
        earlier = jnp.arange(slots)[:, None] > jnp.arange(slots)[None, :]
        repeat = jnp.any(earlier & (local[:, None] == local[None, :]), axis=1)
        used = (live & ~repeat).astype(jnp.int32)
        at = local
    else:
        chain = chain_exchanged(gradient, jacobi_inverse, tiles, local, remote, live)
        at = jnp.arange(blocks, dtype=jnp.int32)
        used = jnp.ones((blocks,), jnp.int32)
    chains = [chain] + [shift(chain, "cols", o) for o in range(1, columns)]

    turn = (BLOCK - width * lax.axis_index("cols")) % BLOCK
    shape = jax.ShapeDtypeStruct
    count = ITERS * (ITERS + 1) // 2
    mixes, plain, smooth, scale = call(
        basis_kernel,
        (
            shape((count * width, BLOCK), f32),
            shape((blocks, (ITERS + 1) * width, BLOCK), f32),
            shape((blocks, ITERS * width, BLOCK), f32),
            shape((8, BLOCK), f32),
        ),
        turn.astype(jnp.int32).reshape(1),
        *pieces,
        jacobi_inverse,
        scalars=1,
    )
    images, precond, gram = call(
        mix_kernel,
        (
            shape((blocks, ITERS * width, BLOCK), f32),
            shape((blocks, ITERS * width, BLOCK), f32),
            shape((1, BLOCK), f32),
        ),
        at,
        used,
        *chains,
        gradient,
        mixes,
        plain,
        smooth,
        jacobi_inverse,
        scalars=2,
        scratch=[
            pltpu.VMEM((blocks, (ITERS + 1) * width, BLOCK), f32),
            pltpu.VMEM(((ITERS + 1) * width, BLOCK), f32),
        ],
    )
    everyone = columns * devices
    grams = lax.all_to_all(
        jnp.broadcast_to(gram[None], (everyone, 1, BLOCK)),
        ("cols", "rows"),
        0,
        0,
        tiled=True,
    )
    return call(
        finish_kernel,
        (shape((width, rows), f32), shape((width, rows), f32)),
        grams,
        scale,
        gradient,
        precond,
        images,
    )


def solution(mesh):
    placed = (
        P("cols", "rows"),
        P(None, "cols"),
        P("rows", None, None),
        P("rows", None, None),
        P("rows", None, None),
        P("rows"),
        P("rows"),
        P("rows"),
    )
    return jax.shard_map(
        on_device,
        mesh=mesh,
        in_specs=placed,
        out_specs=(P("cols", "rows"), P("cols", "rows")),
        check_vma=False,
    )
```

time: 646 us -> 91.3 us (0.14)
  blocking collectives: 284 us -> 12.4 us
  waiting for transfers between devices: 279 us -> 26.6 us
  between operations: 27.4 us -> 1.46 us
  Pallas kernels: 0 us -> 23.5 us
  matrix products: 23.3 us -> 0 us
  other arithmetic: 12 us -> 3.36 us
  starting transfers between devices: 9.95 us -> 17.5 us
    psum x6 -> x0, waiting for transfers between devices: 269 us -> none  [on_device(): lax.psum(jnp.dot(width_factor, (local_part + coupled).reshape(width_dev,...]
    psum x6 -> x0, blocking collectives: 238 us -> none  [the longest x5 198 us: on_device(): lax.psum((jnp.sum(direction * fisher_dir), jnp.sum(fisher_dir * precond_r...]
    all_to_all x5 -> x1, blocking collectives: 46.4 us -> 12.4 us  [on_device(): lax.all_to_all(jnp.broadcast_to(gram[None], (everyone, 1, BLOCK)), ('cols...]
    pallas_call x0 -> x5, Pallas kernels: none -> 23.5 us  [call(): pl.pallas_call(kernel, out_shape=outs, in_specs=specs, out_specs=tuple([V...]
    dot_general x30 -> x0, matrix products: 23.3 us -> none  [the longest x6 8.86 us: precondition(): jnp.einsum('enj,nji->eni', blocks, jacobi_inverse, precision=highest)]
    ppermute x0 -> x10, waiting for transfers between devices: none -> 22.7 us  [the longest x9 22.7 us: shift(): return lax.ppermute(x, axis, [(i, (i - by) % size) for i in range(size)])]
    ppermute x0 -> x10, starting transfers between devices: none -> 14.1 us  [the longest x9 14.1 us: shift(): return lax.ppermute(x, axis, [(i, (i - by) % size) for i in range(size)])]
    reduce_sum x7 -> x2, other arithmetic: 8.86 us -> 0.27 us  [the longest x1 0.19 us: chain_gathered(): jnp.sum(jnp.where(meets, numbers[None, :], 0), axis=1)]
  transfers between devices with their start and end apart: 8 -> 11, of which waited for: 8 -> 4; matrix products, arithmetic and copies ran while one was open for 0% -> 5% of each run, Pallas kernels for 0% -> 17%
where the time goes in v1:
time: 91.3 us; the launch traced here: 90.9 us
  waiting for transfers between devices  26.6 us (29%)
  Pallas kernels  23.5 us (26%)
  starting transfers between devices  17.5 us (19%)
  blocking collectives  12.4 us (14%)
  local copies, waits for them, and re-layouts  6.12 us (7%)
  other arithmetic  3.36 us (4%)
  between operations  1.46 us (2%)
    pallas_call x5, Pallas kernels, call(): pl.pallas_call(kernel, out_shape=outs, in_specs=specs, out_specs=tuple([V...  23.5 us
    ppermute x9, waiting for transfers between devices, shift(): return lax.ppermute(x, axis, [(i, (i - by) % size) for i in range(size)])  22.7 us
    ppermute x9, starting transfers between devices, shift(): return lax.ppermute(x, axis, [(i, (i - by) % size) for i in range(size)])  14.1 us
    all_to_all x1, blocking collectives, on_device(): lax.all_to_all(jnp.broadcast_to(gram[None], (everyone, 1, BLOCK)), ('cols...  12.4 us
    all_to_all x1, waiting for transfers between devices, chain_gathered(): told = lax.all_to_all(told, 'rows', 0, 0, tiled=True)[:, 0]  3.89 us
    unnamed x26, local copies, waits for them, and re-layouts  3.85 us
    all_to_all x1, starting transfers between devices, chain_gathered(): told = lax.all_to_all(told, 'rows', 0, 0, tiled=True)[:, 0]  3.31 us
  transfers between devices with their start and end apart: 11, of which 4 were waited for; matrix products, arithmetic and copies ran while one was open for 5% of the time, Pallas kernels for 17%

profile of v1, /device:TPU:0, one launch (start us, length us, event | category | flops | bytes accessed | tf_op | source)
XLA Modules:
  0.0 90.9 jit_solution(6128699878579494592)
XLA Ops:
  0.6 1.0 %pad_maximum_fusion.1.refs_0_ = f32[32,1152]{1,0:T(8,128)S(1)} fusion(f32[32,128]{1,0:T(8,128)} %bitcast.17, f32[32,1024]{1,0:T(8,128)} %gradient.3), kind=kLoop, calls=%fused_computation.1 | loop fusion | flops 36864 | bytes 294912 | tf_op jit(solution)/shard_map/concatenate | solution.py:329
  1.6 3.0 %collective-permute-start.9 = (f32[32,1152]{1,0:T(8,128)S(1)}, f32[32,1152]{1,0:T(8,128)S(1)}, u32[]{:S(2)}, u32[]{:S(2)}) collective-permute-start(f32[32,1152]{1,0:T(8,128)S(1)} %pad_maximum_fusion.1.refs_0_), channel_id=1, source_target_pairs={{0,8},{8,16},{16,24},{24,0},{1,9},{9,17},{17,25},{25,1},{2,10},{10... | collective-permute-start | bytes 442376 | tf_op jit(solution)/shard_map/ppermute | solution.py:91
  4.6 1.5 %collective-permute-start.8 = (f32[32,1152]{1,0:T(8,128)S(1)}, f32[32,1152]{1,0:T(8,128)S(1)}, u32[]{:S(2)}, u32[]{:S(2)}) collective-permute-start(f32[32,1152]{1,0:T(8,128)S(1)} %pad_maximum_fusion.1.refs_0_), channel_id=1, source_target_pairs={{0,16},{8,24},{16,0},{24,8},{1,17},{9,25},{17,1},{25,9},{2,18},{10... | collective-permute-start | bytes 442376 | tf_op jit(solution)/shard_map/ppermute | solution.py:91
  6.2 0.6 slice.23.tiles
  6.8 2.3 %shard_map.86 = f32[3,160,128]{2,1,0:T(8,128)} custom-call(s32[3]{0:T(128)} %bitcast.19, f32[32,1024]{1,0:T(8,128)} %gradient.3, f32[8,128,128]{2,1,0:T(8,128)} %refs_8_.1, bf16[3,128,128]{2,1,0:T(8,128)(2,1)} %slice.23.tiles), custom_call_target="tpu_custom_call" | custom-call | tf_op jit(solution)/shard_map/pallas_call | solution.py:28
  9.1 1.6 %collective-permute-start.2 = (f32[3,160,128]{2,1,0:T(8,128)}, f32[3,160,128]{2,1,0:T(8,128)S(1)}, u32[]{:S(2)}, u32[]{:S(2)}) collective-permute-start(f32[3,160,128]{2,1,0:T(8,128)} %shard_map.86), channel_id=1, source_target_pairs={{0,2},{1,3},{2,4},{3,5},{4,6},{5,7},{6,0},{7,1},{8,10},{9,11},{10,... | collective-permute-start | bytes 737288 | tf_op jit(solution)/shard_map/ppermute | solution.py:91
  10.7 2.6 %collective-permute-start.1 = (f32[3,160,128]{2,1,0:T(8,128)}, f32[3,160,128]{2,1,0:T(8,128)S(1)}, u32[]{:S(2)}, u32[]{:S(2)}) collective-permute-start(f32[3,160,128]{2,1,0:T(8,128)} %shard_map.86), channel_id=1, source_target_pairs={{0,4},{1,5},{2,6},{3,7},{4,0},{5,1},{6,2},{7,3},{8,12},{9,13},{10,... | collective-permute-start | bytes 737288 | tf_op jit(solution)/shard_map/ppermute | solution.py:91
  13.3 1.4 %collective-permute-start = (f32[3,160,128]{2,1,0:T(8,128)}, f32[3,160,128]{2,1,0:T(8,128)S(1)}, u32[]{:S(2)}, u32[]{:S(2)}) collective-permute-start(f32[3,160,128]{2,1,0:T(8,128)} %shard_map.86), channel_id=1, source_target_pairs={{0,6},{1,7},{2,0},{3,1},{4,2},{5,3},{6,4},{7,5},{8,14},{9,15},{10,... | collective-permute-start | bytes 737288 | tf_op jit(solution)/shard_map/ppermute | solution.py:91
  15.3 0.6 copy-done.10
  16.1 0.6 broadcast_in_dim.34
  16.7 3.3 %all-to-all-start = ((s32[8,1,128]{2,1,0:T(1,128)}), s32[8,1,128]{2,1,0:T(1,128)S(1)}, u32[]{:S(2)}, u32[]{:S(2)}) async-start(s32[8,1,128]{2,1,0:T(1,128)} %broadcast_in_dim.34), calls=%async_computation | async-start | bytes 8192 | tf_op jit(solution)/shard_map/all_to_all | solution.py:114
  20.1 8.9 %collective-permute-done.1 = f32[3,160,128]{2,1,0:T(8,128)S(1)} collective-permute-done((f32[3,160,128]{2,1,0:T(8,128)}, f32[3,160,128]{2,1,0:T(8,128)S(1)}, u32[]{:S(2)}, u32[]{:S(2)}) %collective-permute-start.1) | collective-permute-done | bytes 245792 | tf_op jit(solution)/shard_map/ppermute | solution.py:91
  29.0 1.0 %pad_maximum_fusion.near = f32[4,3,160,128]{3,2,1,0:T(8,128)S(1)} fusion(f32[1,3,160,128]{3,2,1,0:T(8,128)S(1)} %bitcast.14, f32[1,3,160,128]{3,2,1,0:T(8,128)S(1)} %bitcast.15, f32[1,3,160,128]{3,2,1,0:T(8,128)S(1)} %bitcast.16, f32[1,3,160,128]{3,2,1,0:T(8,128)} %bitcast.13), kind=kLoop, calls=%fused_computation | loop fusion | flops 737280 | bytes 1966080 | tf_op jit(solution)/shard_map/stack | solution.py:108
  30.4 3.9 %all-to-all-done = s32[8,1,128]{2,1,0:T(1,128)S(1)} async-done(((s32[8,1,128]{2,1,0:T(1,128)}), s32[8,1,128]{2,1,0:T(1,128)S(1)}, u32[]{:S(2)}, u32[]{:S(2)}) %all-to-all-start) | async-done | bytes 4128 | tf_op jit(solution)/shard_map/all_to_all | solution.py:114
  34.7 0.2 select_reduce_fusion
  35.1 0.6 select_n.57.sources
  35.7 1.0 %copy-done.1 = f32[4,3,160,128]{3,2,1,0:T(8,128)} copy-done((f32[4,3,160,128]{3,2,1,0:T(8,128)}, f32[4,3,160,128]{3,2,1,0:T(8,128)S(1)}, u32[]{:S(2)}) %copy-start.1) | copy-done | bytes 983064
  36.7 5.9 %shard_map.87.refs_0_ = f32[6,3,32,128]{3,2,1,0:T(8,128)} custom-call(s32[72]{0:T(128)} %select_n.57.sources, f32[4,3,160,128]{3,2,1,0:T(8,128)} %copy-done, f32[4,3,160,128]{3,2,1,0:T(8,128)} %copy-done.1), custom_call_target="tpu_custom_call" | custom-call | tf_op jit(solution)/shard_map/pallas_call | solution.py:28
  42.6 0.5 collective-permute-start.6
  43.1 1.5 %collective-permute-start.5 = (f32[6,3,32,128]{3,2,1,0:T(8,128)}, f32[6,3,32,128]{3,2,1,0:T(8,128)S(1)}, u32[]{:S(2)}, u32[]{:S(2)}) collective-permute-start(f32[6,3,32,128]{3,2,1,0:T(8,128)} %shard_map.87.refs_0_), channel_id=1, source_target_pairs={{0,16},{8,24},{16,0},{24,8},{1,17},{9,25},{17,1},{25,9},{2,18},{10... | collective-permute-start | bytes 884744 | tf_op jit(solution)/shard_map/ppermute | solution.py:91
  44.6 1.4 %collective-permute-start.4 = (f32[6,3,32,128]{3,2,1,0:T(8,128)}, f32[6,3,32,128]{3,2,1,0:T(8,128)S(1)}, u32[]{:S(2)}, u32[]{:S(2)}) collective-permute-start(f32[6,3,32,128]{3,2,1,0:T(8,128)} %shard_map.87.refs_0_), channel_id=1, source_target_pairs={{0,24},{8,0},{16,8},{24,16},{1,25},{9,1},{17,9},{25,17},{2,26},{10... | collective-permute-start | bytes 884744 | tf_op jit(solution)/shard_map/ppermute | solution.py:91
  46.0 0.2 fusion.4
  46.2 0.6 collective-permute-start.7
  46.8 0.5 and_convert_fusion.used
  47.3 13.7 %collective-permute-done.7.refs_1_ = f32[32,1152]{1,0:T(8,128)S(1)} collective-permute-done((f32[32,1152]{1,0:T(8,128)S(1)}, f32[32,1152]{1,0:T(8,128)S(1)}, u32[]{:S(2)}, u32[]{:S(2)}) %collective-permute-start.7) | collective-permute-done | bytes 147488 | tf_op jit(solution)/shard_map/ppermute | solution.py:91
  61.0 0.7 copy-done.8
  61.7 6.9 %shard_map.88 = (f32[672,128]{1,0:T(8,128)}, f32[8,224,128]{2,1,0:T(8,128)}, f32[8,192,128]{2,1,0:T(8,128)}, f32[8,128]{1,0:T(8,128)}) custom-call(s32[1]{0:T(128)} %bitcast.6.turn, f32[32,1152]{1,0:T(8,128)} %copy-done.2, f32[32,1152]{1,0:T(8,128)} %copy-done.8, f32[32,1152]{1,0:T(8,128)} %copy-done.7, f32[32,1152]{1,0:T(8,128)} %copy-done.6, ...), custom_call_target="tpu_custom_call" | custom-call | tf_op jit(solution)/shard_map/pallas_call | solution.py:28
  68.6 0.7 copy-done.3
  69.5 5.5 %shard_map.89 = (f32[8,192,128]{2,1,0:T(8,128)}, f32[8,192,128]{2,1,0:T(8,128)}, f32[1,128]{1,0:T(1,128)}) custom-call(s32[3]{0:T(128)} %bitcast.20, s32[3]{0:T(128)} %and_convert_fusion.used, f32[6,3,32,128]{3,2,1,0:T(8,128)} %shard_map.87.refs_0_, f32[6,3,32,128]{3,2,1,0:T(8,128)} %copy-done.5, f32[6,3,32,128]{3,2,1,0:T(8,128)} %copy-done.4, ...), custom_call_target="tpu_custom_call" | custom-call | tf_op jit(solution)/shard_map/pallas_call | solution.py:28
  75.0 0.7 copy-done.11
  75.6 12.4 %all_to_all.10.grams = f32[32,1,128]{2,1,0:T(1,128)} all-to-all(f32[32,1,128]{2,1,0:T(1,128)S(1)} %broadcast_in_dim.67), channel_id=1, replica_groups=mesh['cols'=4,'rows'=8] {'cols','rows'}, dimensions={0} | all-to-all | bytes 32768 | tf_op jit(solution)/shard_map/all_to_all | solution.py:383
  88.1 2.9 %shard_map.90 = (f32[32,1024]{1,0:T(8,128)}, f32[32,1024]{1,0:T(8,128)}) custom-call(f32[32,1,128]{2,1,0:T(1,128)} %all_to_all.10.grams, f32[8,128]{1,0:T(8,128)} %get-tuple-element.13.scale, f32[32,1024]{1,0:T(8,128)} %gradient.3, f32[8,192,128]{2,1,0:T(8,128)} %get-tuple-element.14.precond, f32[8,192,128]{2,1,0:T(8,128)} %get-tuple-element.15.images), custom_call_target="tpu_custom_call" | custom-call | tf_op jit(solution)/shard_map/pallas_call | solution.py:28
  (45 shorter events, 1.4 us)
Async XLA Ops:
  0.6 5.5 %copy-start.9 = (bf16[4,128,128]{2,1,0:T(8,128)(2,1)S(1)}, bf16[4,128,128]{2,1,0:T(8,128)(2,1)}, u32[]{:S(2)}) copy-start(bf16[4,128,128]{2,1,0:T(8,128)(2,1)} %param.11) | copy-start | bytes 393220
  1.6 44.6 %copy-start.2 = (f32[32,1152]{1,0:T(8,128)}, f32[32,1152]{1,0:T(8,128)S(1)}, u32[]{:S(2)}) copy-start(f32[32,1152]{1,0:T(8,128)S(1)} %pad_maximum_fusion.1.refs_0_) | copy-start | bytes 442372
  1.6 44.6 %collective-permute-start.9 = (f32[32,1152]{1,0:T(8,128)S(1)}, f32[32,1152]{1,0:T(8,128)S(1)}, u32[]{:S(2)}, u32[]{:S(2)}) collective-permute-start(f32[32,1152]{1,0:T(8,128)S(1)} %pad_maximum_fusion.1.refs_0_), channel_id=1, source_target_pairs={{0,8},{8,16},{16,24},{24,0},{1,9},{9,17},{17,25},{25,1},{2,10},{10... | collective-permute-start | bytes 442376 | tf_op jit(solution)/shard_map/ppermute | solution.py:91
  4.6 42.7 %collective-permute-start.8 = (f32[32,1152]{1,0:T(8,128)S(1)}, f32[32,1152]{1,0:T(8,128)S(1)}, u32[]{:S(2)}, u32[]{:S(2)}) collective-permute-start(f32[32,1152]{1,0:T(8,128)S(1)} %pad_maximum_fusion.1.refs_0_), channel_id=1, source_target_pairs={{0,16},{8,24},{16,0},{24,8},{1,17},{9,25},{17,1},{25,9},{2,18},{10... | collective-permute-start | bytes 442376 | tf_op jit(solution)/shard_map/ppermute | solution.py:91
  9.1 11.0 %collective-permute-start.2 = (f32[3,160,128]{2,1,0:T(8,128)}, f32[3,160,128]{2,1,0:T(8,128)S(1)}, u32[]{:S(2)}, u32[]{:S(2)}) collective-permute-start(f32[3,160,128]{2,1,0:T(8,128)} %shard_map.86), channel_id=1, source_target_pairs={{0,2},{1,3},{2,4},{3,5},{4,6},{5,7},{6,0},{7,1},{8,10},{9,11},{10,... | collective-permute-start | bytes 737288 | tf_op jit(solution)/shard_map/ppermute | solution.py:91
  10.7 18.3 %collective-permute-start.1 = (f32[3,160,128]{2,1,0:T(8,128)}, f32[3,160,128]{2,1,0:T(8,128)S(1)}, u32[]{:S(2)}, u32[]{:S(2)}) collective-permute-start(f32[3,160,128]{2,1,0:T(8,128)} %shard_map.86), channel_id=1, source_target_pairs={{0,4},{1,5},{2,6},{3,7},{4,0},{5,1},{6,2},{7,3},{8,12},{9,13},{10,... | collective-permute-start | bytes 737288 | tf_op jit(solution)/shard_map/ppermute | solution.py:91
  13.3 15.8 %collective-permute-start = (f32[3,160,128]{2,1,0:T(8,128)}, f32[3,160,128]{2,1,0:T(8,128)S(1)}, u32[]{:S(2)}, u32[]{:S(2)}) collective-permute-start(f32[3,160,128]{2,1,0:T(8,128)} %shard_map.86), channel_id=1, source_target_pairs={{0,6},{1,7},{2,0},{3,1},{4,2},{5,3},{6,4},{7,5},{8,14},{9,15},{10,... | collective-permute-start | bytes 737288 | tf_op jit(solution)/shard_map/ppermute | solution.py:91
  15.3 0.7 copy-start.10
  15.3 0.7 copy-start.12
  16.7 17.6 %all-to-all-start = ((s32[8,1,128]{2,1,0:T(1,128)}), s32[8,1,128]{2,1,0:T(1,128)S(1)}, u32[]{:S(2)}, u32[]{:S(2)}) async-start(s32[8,1,128]{2,1,0:T(1,128)} %broadcast_in_dim.34), calls=%async_computation | async-start | bytes 8192 | tf_op jit(solution)/shard_map/all_to_all | solution.py:114
  30.1 5.6 %copy-start = (f32[4,3,160,128]{3,2,1,0:T(8,128)}, f32[4,3,160,128]{3,2,1,0:T(8,128)S(1)}, u32[]{:S(2)}) copy-start(f32[4,3,160,128]{3,2,1,0:T(8,128)S(1)} %pad_maximum_fusion.near) | copy-start | bytes 2949124
  30.1 5.6 %collective-permute-start.3 = (f32[4,3,160,128]{3,2,1,0:T(8,128)S(1)}, f32[4,3,160,128]{3,2,1,0:T(8,128)S(1)}, u32[]{:S(2)}, u32[]{:S(2)}) collective-permute-start(f32[4,3,160,128]{3,2,1,0:T(8,128)S(1)} %pad_maximum_fusion.near), channel_id=1, source_target_pairs={{0,1},{1,0},{2,3},{3,2},{4,5},{5,4},{6,7},{7,6},{8,9},{9,8},{10,11... | collective-permute-start | bytes 2949128 | tf_op jit(solution)/shard_map/ppermute | solution.py:109
  35.7 1.0 %copy-start.1 = (f32[4,3,160,128]{3,2,1,0:T(8,128)}, f32[4,3,160,128]{3,2,1,0:T(8,128)S(1)}, u32[]{:S(2)}) copy-start(f32[4,3,160,128]{3,2,1,0:T(8,128)S(1)} %collective-permute-done.3.far) | copy-start | bytes 2949124
  42.6 26.0 %collective-permute-start.6 = (f32[6,3,32,128]{3,2,1,0:T(8,128)}, f32[6,3,32,128]{3,2,1,0:T(8,128)S(1)}, u32[]{:S(2)}, u32[]{:S(2)}) collective-permute-start(f32[6,3,32,128]{3,2,1,0:T(8,128)} %shard_map.87.refs_0_), channel_id=1, source_target_pairs={{0,8},{8,16},{16,24},{24,0},{1,9},{9,17},{17,25},{25,1},{2,10},{10... | collective-permute-start | bytes 884744 | tf_op jit(solution)/shard_map/ppermute | solution.py:91
  43.1 25.5 %collective-permute-start.5 = (f32[6,3,32,128]{3,2,1,0:T(8,128)}, f32[6,3,32,128]{3,2,1,0:T(8,128)S(1)}, u32[]{:S(2)}, u32[]{:S(2)}) collective-permute-start(f32[6,3,32,128]{3,2,1,0:T(8,128)} %shard_map.87.refs_0_), channel_id=1, source_target_pairs={{0,16},{8,24},{16,0},{24,8},{1,17},{9,25},{17,1},{25,9},{2,18},{10... | collective-permute-start | bytes 884744 | tf_op jit(solution)/shard_map/ppermute | solution.py:91
  44.6 24.0 %collective-permute-start.4 = (f32[6,3,32,128]{3,2,1,0:T(8,128)}, f32[6,3,32,128]{3,2,1,0:T(8,128)S(1)}, u32[]{:S(2)}, u32[]{:S(2)}) collective-permute-start(f32[6,3,32,128]{3,2,1,0:T(8,128)} %shard_map.87.refs_0_), channel_id=1, source_target_pairs={{0,24},{8,0},{16,8},{24,16},{1,25},{9,1},{17,9},{25,17},{2,26},{10... | collective-permute-start | bytes 884744 | tf_op jit(solution)/shard_map/ppermute | solution.py:91
  46.2 14.8 %copy-start.6 = (f32[32,1152]{1,0:T(8,128)}, f32[32,1152]{1,0:T(8,128)S(1)}, u32[]{:S(2)}) copy-start(f32[32,1152]{1,0:T(8,128)S(1)} %collective-permute-done.9.refs_3_) | copy-start | bytes 442372
  46.2 14.8 %collective-permute-start.7 = (f32[32,1152]{1,0:T(8,128)S(1)}, f32[32,1152]{1,0:T(8,128)S(1)}, u32[]{:S(2)}, u32[]{:S(2)}) collective-permute-start(f32[32,1152]{1,0:T(8,128)S(1)} %pad_maximum_fusion.1.refs_0_), channel_id=1, source_target_pairs={{0,24},{8,0},{16,8},{24,16},{1,25},{9,1},{17,9},{25,17},{2,26},{10... | collective-permute-start | bytes 442376 | tf_op jit(solution)/shard_map/ppermute | solution.py:91
  47.3 13.7 %copy-start.7 = (f32[32,1152]{1,0:T(8,128)}, f32[32,1152]{1,0:T(8,128)S(1)}, u32[]{:S(2)}) copy-start(f32[32,1152]{1,0:T(8,128)S(1)} %collective-permute-done.8.refs_2_) | copy-start | bytes 442372
  61.0 0.7 copy-start.8
  68.6 0.7 copy-start.3
  68.6 0.8 copy-start.4
  68.6 0.9 copy-start.5
  75.0 0.7 copy-start.11
